TPU v7x, 512 devices: a whole 4x4x16 slice. The times are simulated.
512 devices in a mesh: section: 32 (over z, core), seq: 16 (over x, y).
Axes of the slice: x: 4, y: 4, z: 16, core: 2. Of those that a mesh axis runs over, the one named last changes fastest.
Arguments:
- layer_input: bfloat16 [32, 3, 4096, 768], P('section', None, 'seq'), may hold values from -6 to 6
- grad_out: bfloat16 [32, 3, 4096, 768], P('section', None, 'seq'), may hold values from -6 to 6
- gate_weight: bfloat16 [768, 768], P('seq'), may hold values from -0.21875 to 0.21875
- mix_in_right: bfloat16 [64, 64, 64], P('seq'), may hold values from -0.75 to 0.75
- mix_in_left: bfloat16 [64, 64, 64], P('seq'), may hold values from -0.75 to 0.75
- mix_out_left: bfloat16 [64, 64, 64], P('seq'), may hold values from -0.75 to 0.75
- mix_out_right: bfloat16 [64, 64, 64], P('seq'), may hold values from -0.75 to 0.75
- kernel: bfloat16 [4096, 768], P('seq'), may hold values from -5 to 5
Outputs:
- input_grad: bfloat16 [32, 3, 4096, 768], P('section', None, 'seq')
- weight_grad: float32 [768, 768], P('seq')
- kernel_grad: bfloat16 [4096, 768], P('seq')
All inputs are finite; a program needn't handle non-finite values.
Results may differ from a plain program's by a relative error of at most 0.007.
Values may be sent and summed in bfloat16 or wider, within the bound.
A program may use at most 64 MiB of HBM per device.

v0:
```python
import math
import jax
import jax.numpy as jnp
from jax import lax
from jax.sharding import PartitionSpec as P

BATCH = 3
SEQ = 4096


def contract(form, left, right):
    return jnp.einsum(form, left, right, preferred_element_type=jnp.float32)


def forward_middle(spread, left_in, left_out, kern):
    second_mixed = contract("ija,baid->bijd", left_in, spread)
    weighted = (second_mixed * kern).astype(jnp.bfloat16)
    third_mixed = contract("ikj,bijd->bikd", left_out, weighted).astype(jnp.bfloat16)
    return (second_mixed, third_mixed)


def backward_middle(back_spread, second_mixed, left_in, left_out, kern):
    back_second = contract("ikj,bkid->bijd", left_out, back_spread)
    kernel_sum = jnp.sum(second_mixed * back_second, axis=0)
    back_weighted = (back_second * kern).astype(jnp.bfloat16)
    back_first = contract("ija,bijd->biad", left_in, back_weighted).astype(jnp.bfloat16)
    return (kernel_sum, back_first)


def local(
    layer_input,
    grad_out,
    gate_weight,
    mix_in_right,
    mix_in_left,
    mix_out_left,
    mix_out_right,
    kernel,
):
    count_batch = layer_input.shape[1]
    token_rows = layer_input.shape[2]
    width = layer_input.shape[3]
    groups = mix_in_right.shape[0]
    block_size = mix_in_right.shape[1]
    replicas = lax.axis_size("section")
    kern = kernel.reshape(groups, block_size, width).astype(jnp.float32)
    acts = layer_input[0].reshape(count_batch, groups, block_size, width)
    flat_input = layer_input[0].reshape(count_batch * token_rows, width)
    upstream = grad_out[0].reshape(count_batch * token_rows, width).astype(jnp.float32)
    weights = lax.all_gather(gate_weight, "seq", axis=0, tiled=True)
    preact = jnp.dot(flat_input, weights, preferred_element_type=jnp.float32)
    sigma = jax.nn.sigmoid(preact)
    swish = preact * sigma
    slope = sigma * (1.0 + preact * (1.0 - sigma))
    mix_grad = (
        (upstream * swish).astype(jnp.bfloat16).reshape(count_batch, groups, block_size, width)
    )
    first_mixed = contract("aic,bacd->baid", mix_in_right, acts).astype(jnp.bfloat16)
    back_third = contract("kmi,bkmd->bkid", mix_out_right, mix_grad).astype(jnp.bfloat16)
    spread = lax.all_to_all(first_mixed, "seq", split_axis=2, concat_axis=1, tiled=True)
    second_mixed, third_mixed = forward_middle(spread, mix_in_left, mix_out_left, kern)
    returned = lax.all_to_all(third_mixed, "seq", split_axis=2, concat_axis=1, tiled=True)
    back_spread = lax.all_to_all(back_third, "seq", split_axis=2, concat_axis=1, tiled=True)
    kernel_sum, back_first = backward_middle(
        back_spread, second_mixed, mix_in_left, mix_out_left, kern
    )
    back_return = lax.all_to_all(back_first, "seq", split_axis=2, concat_axis=1, tiled=True)
    mixed = contract("kmi,bikd->bkmd", mix_out_right, returned).reshape(
        count_batch * token_rows, width
    )
    gate_grad = (upstream * mixed * slope).astype(jnp.bfloat16)
    gate_part = lax.dot_general(
        gate_grad, weights, (((1,), (1,)), ((), ())), preferred_element_type=jnp.float32
    )
    weight_scale = 1.0 / math.sqrt(replicas * BATCH * SEQ)
    kernel_scale = 1.0 / math.sqrt(replicas * BATCH)
    term = lax.dot_general(
        flat_input, gate_grad, (((0,), (0,)), ((), ())), preferred_element_type=jnp.float32
    )
    weight_local = lax.psum_scatter(term * weight_scale, "seq", scatter_dimension=0, tiled=True)
    weight_grad, kernel_total = lax.psum((weight_local, kernel_sum * kernel_scale), "section")
    mix_part = contract("aic,biad->bacd", mix_in_right, back_return).reshape(
        count_batch * token_rows, width
    )
    input_grad = (
        (gate_part + mix_part).astype(jnp.bfloat16).reshape(1, count_batch, token_rows, width)
    )
    kernel_grad = kernel_total.astype(jnp.bfloat16).reshape(groups * block_size, width)
    return (input_grad, weight_grad, kernel_grad)


def solution(mesh):
    placed = (
        P("section", None, "seq", None),
        P("section", None, "seq", None),
        P("seq", None),
        P("seq", None, None),
        P("seq", None, None),
        P("seq", None, None),
        P("seq", None, None),
        P("seq", None),
    )
    return jax.shard_map(
        local,
        mesh=mesh,
        in_specs=placed,
        out_specs=(P("section", None, "seq", None), P("seq", None), P("seq", None)),
        check_vma=False,
    )
```

profile of v0, /device:TPU:2, one launch (start us, length us, event | category | flops | bytes accessed | tf_op | source)
XLA Modules:
  0.0 457.6 jit_solution(12352171297710613128)
XLA Ops:
  7.2 1.3 copy-done
  8.4 1.3 fusion.9
  9.7 1.9 copy.54
  11.7 9.5 %all-to-all-start = ((bf16[3,4,64,768]{3,1,0,2:T(4,128)(2,1)}), bf16[3,4,64,768]{3,1,0,2:T(4,128)(2,1)S(1)}, u32[]{:S(2)}, u32[]{:S(2)}) async-start(bf16[3,4,64,768]{3,1,0,2:T(4,128)(2,1)} %copy.54), calls=%async_computation | async-start | bytes 2359296 | tf_op jit(solution)/shard_map/all_to_all | solution.py:60
  22.0 0.9 convert.3
  22.9 13.2 %all-to-all-done = bf16[3,4,64,768]{3,1,0,2:T(4,128)(2,1)S(1)} async-done(((bf16[3,4,64,768]{3,1,0,2:T(4,128)(2,1)}), bf16[3,4,64,768]{3,1,0,2:T(4,128)(2,1)S(1)}, u32[]{:S(2)}, u32[]{:S(2)}) %all-to-all-start) | async-done | bytes 1179680 | tf_op jit(solution)/shard_map/all_to_all | solution.py:60
  36.6 1.2 all_to_all.55
  37.8 1.8 fusion.23
  41.1 22.2 %all_to_all.72 = bf16[3,4,64,768]{3,1,0,2:T(4,128)(2,1)S(1)} all-to-all(bf16[3,4,64,768]{3,1,0,2:T(4,128)(2,1)S(1)} %copy.56), channel_id=1, replica_groups=mesh['section'=32,'seq'=16] {'seq'}, dimensions={2} | all-to-all | bytes 2359296 | tf_op jit(solution)/shard_map/all_to_all | solution.py:62
  63.2 1.5 copy.98
  64.8 3.1 all_to_all.59
  67.9 1.8 convolution_bitcast_fusion
  69.7 1.6 copy.58
  71.2 18.5 %all-gather.2.cloned.1.call-done = bf16[768,768]{1,0:T(8,128)(2,1)} async-done(((bf16[48,768]{1,0:T(8,128)(2,1)}), bf16[768,768]{1,0:T(8,128)(2,1)}) %all-gather.2.cloned.1.call-update) | async-done | bytes 1179664 | tf_op jit(solution)/shard_map/all_gather | solution.py:50
  89.7 5.1 %fusion.1 = (bf16[768,768]{1,0:T(8,128)(2,1)S(1)}, bf16[768,768]{1,0:T(8,128)(2,1)}) fusion(f32[3,4,64,768]{3,2,1,0:T(8,128)} %copy.58, bf16[1,3,256,768]{3,2,1,0:T(8,128)(2,1)} %param.9, bf16[768,768]{1,0:T(8,128)(2,1)S(1)} %bitcast.123, bf16[768,768]{1,0:T(8,128)(2,1)} %all-gather.2.cloned.1.call-done), kind=kOutput, calls=%fused_computation.3 | convolution fusion | flops 914227200 | bytes 8257536 | tf_op jit(solution)/shard_map/dot_general | solution.py:51
  94.9 1.1 copy-done.7
  95.9 2.5 multiply_bitcast_fusion
  98.4 3.1 copy.86
  101.5 1.8 fusion.7
  104.2 22.5 %all_to_all.73 = bf16[3,4,64,768]{3,1,0,2:T(4,128)(2,1)S(1)} all-to-all(bf16[3,4,64,768]{3,1,0,2:T(4,128)(2,1)S(1)} %copy.61), channel_id=1, replica_groups=mesh['section'=32,'seq'=16] {'seq'}, dimensions={2} | all-to-all | bytes 2359296 | tf_op jit(solution)/shard_map/all_to_all | solution.py:63
  126.8 1.5 copy.97
  128.3 3.2 all_to_all.63
  131.5 2.8 fusion.5
  134.8 1.9 copy.65
  136.8 5.5 %all-to-all-start.3 = ((bf16[3,4,64,768]{3,1,0,2:T(4,128)(2,1)}), bf16[3,4,64,768]{3,1,0,2:T(4,128)(2,1)S(1)}, u32[]{:S(2)}, u32[]{:S(2)}) async-start(bf16[3,4,64,768]{3,1,0,2:T(4,128)(2,1)} %copy.65), calls=%async_computation.3 | async-start | bytes 2359296 | tf_op jit(solution)/shard_map/all_to_all | solution.py:67
  142.3 1.0 broadcast_multiply_fusion
  143.2 100.1 %all-reduce.4 = bf16[4,64,768]{2,1,0:T(8,128)(2,1)} all-reduce(f32[4,64,768]{2,1,0:T(8,128)} %broadcast_multiply_fusion), channel_id=1, replica_groups=mesh['section'=32,'seq'=16] {'section'}, use_global_device_ids=true, to_apply=%region_3.0 | all-reduce | flops 196608 | bytes 1179648 | tf_op jit(solution)/shard_map/psum | solution.py:81
  244.2 1.4 convolution_bitcast_fusion.1
  245.7 1.8 copy.87
  247.6 3.8 fusion.3
  251.3 198.0 %all-reduce.3.cloned.1.call-done = f32[48,768]{0,1:T(8,128)} async-done(((f32[48,768]{0,1:T(8,128)}), f32[48,768]{0,1:T(8,128)}) %all-reduce.3.cloned.1.call-update) | async-done | bytes 147472 | tf_op jit(solution)/shard_map/psum | solution.py:81
  449.3 1.8 copy.69
  (30 shorter events, 5.2 us)
Async XLA Ops:
  7.2 1.3 copy-start
  11.7 10.3 %copy-start.4 = (bf16[256,768]{1,0:T(8,128)(2,1)S(1)}, bf16[256,768]{1,0:T(8,128)(2,1)}, u32[]{:S(2)}) copy-start(bf16[256,768]{1,0:T(8,128)(2,1)} %param.15) | copy-start | bytes 1179652
  11.7 24.5 %all-to-all-start = ((bf16[3,4,64,768]{3,1,0,2:T(4,128)(2,1)}), bf16[3,4,64,768]{3,1,0,2:T(4,128)(2,1)S(1)}, u32[]{:S(2)}, u32[]{:S(2)}) async-start(bf16[3,4,64,768]{3,1,0,2:T(4,128)(2,1)} %copy.54), calls=%async_computation | async-start | bytes 2359296 | tf_op jit(solution)/shard_map/all_to_all | solution.py:60
  21.2 68.5 %all-gather.2.cloned.1.call-start = ((), (), s32[]{:S(2)}) async-start(), calls=%async_computation.5 | async-start | bytes 1253376 | tf_op jit(solution)/shard_map/all_gather | solution.py:50
  21.9 223.8 %reduce-scatter.4.cloned.1.call-start = ((), (), s32[]{:S(2)}) async-start(), calls=%async_computation.7 | async-start | bytes 2506752
  37.8 1.8 copy-start.1
  37.8 1.8 copy-start.5
  94.9 1.1 copy-start.7
  131.5 2.8 copy-start.2
  131.5 2.8 copy-start.6
  136.8 5.5 %copy-start.3 = (f32[4,64,768]{2,1,0:T(8,128)S(1)}, f32[4,64,768]{2,1,0:T(8,128)}, u32[]{:S(2)}) copy-start(f32[4,64,768]{2,1,0:T(8,128)} %get-tuple-element.17) | copy-start | bytes 2359300
  136.8 106.6 %all-to-all-start.3 = ((bf16[3,4,64,768]{3,1,0,2:T(4,128)(2,1)}), bf16[3,4,64,768]{3,1,0,2:T(4,128)(2,1)S(1)}, u32[]{:S(2)}, u32[]{:S(2)}) async-start(bf16[3,4,64,768]{3,1,0,2:T(4,128)(2,1)} %copy.65), calls=%async_computation.3 | async-start | bytes 2359296 | tf_op jit(solution)/shard_map/all_to_all | solution.py:67
  142.2 307.1 %all-reduce.3.cloned.1.call-start = ((), (), s32[]{:S(2)}) async-start(), calls=%async_computation.6 | async-start | bytes 786432 | tf_op jit(solution)/shard_map/psum | solution.py:81
Sparse Core Ops, SparseCore 0:
  25.1 64.5 all-gather.1
  101.6 98.0 reduce-scatter.3
  247.7 201.5 all-reduce.2
where the time goes:
time: 459 us; the launch traced here: 458 us
  waiting for transfers between devices  230 us (50%)
  blocking collectives  145 us (32%)
  local copies, waits for them, and re-layouts  28.3 us (6%)
  matrix products  23.3 us (5%)
  starting transfers between devices  15.1 us (3%)
  between operations  13.9 us (3%)
    psum x1, waiting for transfers between devices, local(): lax.psum((weight_local, kernel_sum * kernel_scale), 'section')  198 us
    psum x1, blocking collectives, local(): lax.psum((weight_local, kernel_sum * kernel_scale), 'section')  100 us
    all_to_all x1, blocking collectives, local(): lax.all_to_all(back_third, 'seq', split_axis=2, concat_axis=1, tiled=True)  22.5 us
    all_to_all x1, blocking collectives, local(): lax.all_to_all(third_mixed, 'seq', split_axis=2, concat_axis=1, tiled=True)  22.2 us
    all_gather x1, waiting for transfers between devices, local(): weights = lax.all_gather(gate_weight, 'seq', axis=0, tiled=True)  18.5 us
    all_to_all x1, waiting for transfers between devices, local(): lax.all_to_all(first_mixed, 'seq', split_axis=2, concat_axis=1, tiled=True)  13.2 us
    dot_general x8, matrix products, contract(): return jnp.einsum(form, left, right, preferred_element_type=jnp.float32)  11.8 us
    all_to_all x1, starting transfers between devices, local(): lax.all_to_all(first_mixed, 'seq', split_axis=2, concat_axis=1, tiled=True)  9.55 us
  transfers between devices with their start and end apart: 5, of which 3 were waited for; matrix products, arithmetic and copies ran while one was open for 6% of the time, Pallas kernels for 0%

commit v1 on v0

--- a/solution.py
+++ b/solution.py
@@ -59,7 +59,12 @@
     back_third = contract("kmi,bkmd->bkid", mix_out_right, mix_grad).astype(jnp.bfloat16)
     spread = lax.all_to_all(first_mixed, "seq", split_axis=2, concat_axis=1, tiled=True)
     second_mixed, third_mixed = forward_middle(spread, mix_in_left, mix_out_left, kern)
-    returned = lax.all_to_all(third_mixed, "seq", split_axis=2, concat_axis=1, tiled=True)
+    returned = jnp.concatenate(
+        lax.all_to_all(
+            jnp.stack(jnp.split(third_mixed, lax.axis_size("seq"), axis=2), axis=0), "seq", 0, 0
+        ),
+        axis=1,
+    )
     back_spread = lax.all_to_all(back_third, "seq", split_axis=2, concat_axis=1, tiled=True)
     kernel_sum, back_first = backward_middle(
         back_spread, second_mixed, mix_in_left, mix_out_left, kern

time: 459 us -> 459 us (level)
  waiting for transfers between devices: 230 us -> 236 us
  local copies, waits for them, and re-layouts: 28.3 us -> 23.4 us
    all_gather x1, waiting for transfers between devices: 18.5 us -> 24.6 us  [local(): weights = lax.all_gather(gate_weight, 'seq', axis=0, tiled=True)]
    all_to_all x2 -> x0, local copies, waits for them, and re-layouts: 4.69 us -> none  [local(): lax.all_to_all(third_mixed, 'seq', split_axis=2, concat_axis=1, tiled=True)]
    unnamed x19 -> x36, local copies, waits for them, and re-layouts: 9.03 us -> 9.72 us
  transfers between devices with their start and end apart: 5 -> 5, of which waited for: 3 -> 3; matrix products, arithmetic and copies ran while one was open for 6% -> 5% of each run, Pallas kernels for 0% -> 0%
where the time goes in v1:
time: 459 us; the launch traced here: 458 us
  waiting for transfers between devices  236 us (51%)
  blocking collectives  146 us (32%)
  local copies, waits for them, and re-layouts  23.4 us (5%)
  matrix products  22 us (5%)
  starting transfers between devices  15.1 us (3%)
  between operations  13.9 us (3%)
    psum x1, waiting for transfers between devices, local(): lax.psum((weight_local, kernel_sum * kernel_scale), 'section')  197 us
    psum x1, blocking collectives, local(): lax.psum((weight_local, kernel_sum * kernel_scale), 'section')  101 us
    all_gather x1, waiting for transfers between devices, local(): weights = lax.all_gather(gate_weight, 'seq', axis=0, tiled=True)  24.6 us
    all_to_all x1, blocking collectives, local(): lax.all_to_all(back_third, 'seq', split_axis=2, concat_axis=1, tiled=True)  22.5 us
    all_to_all x1, blocking collectives, local(): lax.all_to_all(jnp.stack(jnp.split(third_mixed, lax.axis_size('seq'), axi...  22.3 us
    all_to_all x1, waiting for transfers between devices, local(): lax.all_to_all(first_mixed, 'seq', split_axis=2, concat_axis=1, tiled=True)  13.2 us
    dot_general x8, matrix products, contract(): return jnp.einsum(form, left, right, preferred_element_type=jnp.float32)  10.5 us
    unnamed x36, local copies, waits for them, and re-layouts  9.72 us
  transfers between devices with their start and end apart: 5, of which 3 were waited for; matrix products, arithmetic and copies ran while one was open for 5% of the time, Pallas kernels for 0%

profile of v1, /device:TPU:2, one launch (start us, length us, event | category | flops | bytes accessed | tf_op | source)
XLA Modules:
  0.0 458.2 jit_solution(2591197787290859556)
XLA Ops:
  7.2 1.3 copy-done
  8.4 1.3 fusion.9
  9.7 1.9 copy.53
  11.7 9.5 %all-to-all-start = ((bf16[3,4,64,768]{3,1,0,2:T(4,128)(2,1)}), bf16[3,4,64,768]{3,1,0,2:T(4,128)(2,1)S(1)}, u32[]{:S(2)}, u32[]{:S(2)}) async-start(bf16[3,4,64,768]{3,1,0,2:T(4,128)(2,1)} %copy.53), calls=%async_computation | async-start | bytes 2359296 | tf_op jit(solution)/shard_map/all_to_all | solution.py:60
  21.2 0.7 all-gather.2.cloned.1.call-update
  22.0 1.0 convert.3
  22.9 13.2 %all-to-all-done = bf16[3,4,64,768]{3,1,0,2:T(4,128)(2,1)S(1)} async-done(((bf16[3,4,64,768]{3,1,0,2:T(4,128)(2,1)}), bf16[3,4,64,768]{3,1,0,2:T(4,128)(2,1)S(1)}, u32[]{:S(2)}, u32[]{:S(2)}) %all-to-all-start) | async-done | bytes 1179680 | tf_op jit(solution)/shard_map/all_to_all | solution.py:60
  36.6 1.2 all_to_all.45
  37.8 1.8 fusion.40
  40.9 22.3 %all_to_all.59 = bf16[16,3,4,4,768]{4,3,1,2,0:T(4,128)(2,1)S(1)} all-to-all(bf16[16,3,4,4,768]{4,3,1,2,0:T(4,128)(2,1)S(1)} %fusion.18), channel_id=1, replica_groups=mesh['section'=32,'seq'=16] {'seq'}, dimensions={0} | all-to-all | bytes 2359296 | tf_op jit(solution)/shard_map/all_to_all | solution.py:63
  63.7 1.6 copy.56
  65.2 24.6 %all-gather.2.cloned.1.call-done = bf16[768,768]{1,0:T(8,128)(2,1)} async-done(((bf16[48,768]{1,0:T(8,128)(2,1)}), bf16[768,768]{1,0:T(8,128)(2,1)}) %all-gather.2.cloned.1.call-update) | async-done | bytes 1179664 | tf_op jit(solution)/shard_map/all_gather | solution.py:50
  89.8 5.1 %fusion.1 = (bf16[768,768]{1,0:T(8,128)(2,1)S(1)}, bf16[768,768]{1,0:T(8,128)(2,1)}) fusion(f32[3,4,64,768]{3,2,1,0:T(8,128)} %copy.56, bf16[1,3,256,768]{3,2,1,0:T(8,128)(2,1)} %param.9, bf16[768,768]{1,0:T(8,128)(2,1)S(1)} %bitcast.183, bf16[768,768]{1,0:T(8,128)(2,1)} %all-gather.2.cloned.1.call-done), kind=kOutput, calls=%fused_computation.3 | convolution fusion | flops 914227200 | bytes 8257536 | tf_op jit(solution)/shard_map/dot_general | solution.py:51
  95.0 1.1 copy-done.8
  96.1 2.5 multiply_bitcast_fusion
  98.6 3.1 copy.84
  101.7 1.8 fusion.7
  103.5 0.9 copy.59
  104.4 22.5 %all_to_all.60 = bf16[3,4,64,768]{3,1,0,2:T(4,128)(2,1)S(1)} all-to-all(bf16[3,4,64,768]{3,1,0,2:T(4,128)(2,1)S(1)} %copy.59), channel_id=1, replica_groups=mesh['section'=32,'seq'=16] {'seq'}, dimensions={2} | all-to-all | bytes 2359296 | tf_op jit(solution)/shard_map/all_to_all | solution.py:68
  126.9 1.5 copy.96
  128.4 3.2 all_to_all.50
  131.6 2.8 fusion.5
  134.4 0.5 fusion.8
  135.0 1.9 copy.63
  136.9 5.5 %all-to-all-start.3 = ((bf16[3,4,64,768]{3,1,0,2:T(4,128)(2,1)}), bf16[3,4,64,768]{3,1,0,2:T(4,128)(2,1)S(1)}, u32[]{:S(2)}, u32[]{:S(2)}) async-start(bf16[3,4,64,768]{3,1,0,2:T(4,128)(2,1)} %copy.63), calls=%async_computation.3 | async-start | bytes 2359296 | tf_op jit(solution)/shard_map/all_to_all | solution.py:72
  142.4 1.0 broadcast_multiply_fusion
  143.4 101.1 %all-reduce.4 = bf16[4,64,768]{2,1,0:T(8,128)(2,1)} all-reduce(f32[4,64,768]{2,1,0:T(8,128)} %broadcast_multiply_fusion), channel_id=1, replica_groups=mesh['section'=32,'seq'=16] {'section'}, use_global_device_ids=true, to_apply=%region_3.0 | all-reduce | flops 196608 | bytes 1179648 | tf_op jit(solution)/shard_map/psum | solution.py:86
  245.4 1.4 convolution_bitcast_fusion.1
  246.9 1.8 copy.85
  248.8 3.8 fusion.3
  252.5 197.3 %all-reduce.3.cloned.1.call-done = f32[48,768]{0,1:T(8,128)} async-done(((f32[48,768]{0,1:T(8,128)}), f32[48,768]{0,1:T(8,128)}) %all-reduce.3.cloned.1.call-update) | async-done | bytes 147472 | tf_op jit(solution)/shard_map/psum | solution.py:86
  449.8 1.8 copy.67
  (45 shorter events, 3.3 us)
Async XLA Ops:
  7.2 1.3 copy-start
  11.7 10.3 %copy-start.4 = (bf16[256,768]{1,0:T(8,128)(2,1)S(1)}, bf16[256,768]{1,0:T(8,128)(2,1)}, u32[]{:S(2)}) copy-start(bf16[256,768]{1,0:T(8,128)(2,1)} %param.15) | copy-start | bytes 1179652
  11.7 24.5 %all-to-all-start = ((bf16[3,4,64,768]{3,1,0,2:T(4,128)(2,1)}), bf16[3,4,64,768]{3,1,0,2:T(4,128)(2,1)S(1)}, u32[]{:S(2)}, u32[]{:S(2)}) async-start(bf16[3,4,64,768]{3,1,0,2:T(4,128)(2,1)} %copy.53), calls=%async_computation | async-start | bytes 2359296 | tf_op jit(solution)/shard_map/all_to_all | solution.py:60
  21.2 68.6 %all-gather.2.cloned.1.call-start = ((), (), s32[]{:S(2)}) async-start(), calls=%async_computation.5 | async-start | bytes 1253376 | tf_op jit(solution)/shard_map/all_gather | solution.py:50
  21.9 225.0 %reduce-scatter.4.cloned.1.call-start = ((), (), s32[]{:S(2)}) async-start(), calls=%async_computation.7 | async-start | bytes 2506752
  37.8 1.8 copy-start.1
  37.8 1.8 copy-start.5
  40.9 22.3 %copy-start.7 = (bf16[4,64,64]{2,1,0:T(8,128)(2,1)S(1)}, bf16[4,64,64]{2,1,0:T(8,128)(2,1)}, u32[]{:S(2)}) copy-start(bf16[4,64,64]{2,1,0:T(8,128)(2,1)} %param.14) | copy-start | bytes 98308
  95.0 1.1 copy-start.8
  131.6 2.8 copy-start.2
  131.6 2.8 copy-start.6
  136.9 5.5 %copy-start.3 = (f32[4,64,768]{2,1,0:T(8,128)S(1)}, f32[4,64,768]{2,1,0:T(8,128)}, u32[]{:S(2)}) copy-start(f32[4,64,768]{2,1,0:T(8,128)} %get-tuple-element.17) | copy-start | bytes 2359300
  136.9 107.6 %all-to-all-start.3 = ((bf16[3,4,64,768]{3,1,0,2:T(4,128)(2,1)}), bf16[3,4,64,768]{3,1,0,2:T(4,128)(2,1)S(1)}, u32[]{:S(2)}, u32[]{:S(2)}) async-start(bf16[3,4,64,768]{3,1,0,2:T(4,128)(2,1)} %copy.63), calls=%async_computation.3 | async-start | bytes 2359296 | tf_op jit(solution)/shard_map/all_to_all | solution.py:72
  142.4 307.5 %all-reduce.3.cloned.1.call-start = ((), (), s32[]{:S(2)}) async-start(), calls=%async_computation.6 | async-start | bytes 786432 | tf_op jit(solution)/shard_map/psum | solution.py:86
Sparse Core Ops, SparseCore 0:
  25.1 64.6 all-gather.1
  101.8 97.1 reduce-scatter.3
  248.9 200.9 all-reduce.2
